TPU v7x, 32 devices: a whole 2x2x4 slice. The times are simulated.
32 devices in a mesh: real: 4 (over y, core), sky: 8 (over z, x).
Axes of the slice: x: 2, y: 2, z: 4, core: 2. Of those that a mesh axis runs over, the one named last changes fastest.
Arguments:
- potential_stock: bfloat16 [8, 256, 16384], P('real', 'sky'), may hold values from -6 to 6
- plane_pick: int32 [4], replicated, may hold values from 0 to 7, as said below
- col_shift: int32 [4, 4], P('real'), may hold values from 0 to 16383
- mirror: int32 [4, 4], P('real'), may hold values from 0 to 1
- subcell: int32 [32, 16], P('sky'), may hold values from 0 to 15
- lens_weight: float32 [4], replicated, may hold values from 0.02 to 0.08
Outputs:
- deflect: float32 [2, 4, 256, 2048], P(None, 'real', 'sky')
- distort: float32 [4, 4, 256, 2048], P(None, 'real', 'sky')
Inputs may be any that keep to these rules, and one draw needn't show every extreme that they name: `plane_pick`: the 4 entries are distinct stored entries; entry q is held by the realization group q // 2.
All inputs are finite; a program needn't handle non-finite values.
Results may differ from a plain program's by a relative error of at most 0.0003.
Values may be sent and summed in bfloat16 or wider, within the bound.
A program may use at most 64 MiB of HBM per device.

v0:
```python
import jax
import jax.numpy as jnp
from jax import lax
from jax.sharding import PartitionSpec as P

PLANES = 4
SUB = 4
TILE_R = 8
TILE_C = 128


first_coef = (1.0 / 12.0, -8.0 / 12.0, 0.0, 8.0 / 12.0, -1.0 / 12.0)
second_coef = (-1.0 / 12.0, 16.0 / 12.0, -30.0 / 12.0, 16.0 / 12.0, -1.0 / 12.0)


def extended_2(x, sides, width):
    for axis, dim in sides:
        peers, length = (lax.axis_size(axis), x.shape[dim])
        up = [(i, (i + 1) % peers) for i in range(peers)]
        down = [(j, i) for i, j in up]
        last = lax.slice_in_dim(x, length - width, length, axis=dim)
        first = lax.slice_in_dim(x, 0, width, axis=dim)
        before = lax.ppermute(last, axis, up)
        after = lax.ppermute(first, axis, down)
        x = jnp.concatenate([before, x, after], axis=dim)
    return x


def spread(value, axis, source):
    kept = jnp.where(lax.axis_index(axis) == source, value, 0).astype(value.dtype)
    return lax.psum(kept, axis)


def cubic_weights(frac):
    sq = frac * frac
    cube = sq * frac
    return (
        (-cube + 2.0 * sq - frac) * 0.5,
        (3.0 * cube - 5.0 * sq + 2.0) * 0.5,
        (-3.0 * cube + 4.0 * sq + frac) * 0.5,
        (cube - sq) * 0.5,
    )


def tap_weights(subcell):
    frac_x = ((subcell % SUB).astype(jnp.float32) + 0.5) / SUB
    frac_y = ((subcell // SUB).astype(jnp.float32) + 0.5) / SUB
    weights_x = tuple((w[:, None, :, None] for w in cubic_weights(frac_x)))
    weights_y = tuple((w[:, None, :, None] for w in cubic_weights(frac_y)))
    return (weights_x, weights_y)


def derivatives(tile):
    nrows = tile.shape[0] - 5
    ncols = tile.shape[1] - 5

    def window(drow, dcol):
        return tile[3 + drow : 3 + drow + nrows, 3 + dcol : 3 + dcol + ncols]

    grad_x = sum((first_coef[q] * window(0, q - 2) for q in range(5) if q != 2))
    grad_y = sum((first_coef[q] * window(q - 2, 0) for q in range(5) if q != 2))
    hess_xx = sum((second_coef[q] * window(0, q - 2) for q in range(5)))
    hess_yy = sum((second_coef[q] * window(q - 2, 0) for q in range(5)))
    hess_xy = sum(
        (
            first_coef[p] * first_coef[q] * window(p - 2, q - 2)
            for p in range(5)
            for q in range(5)
            if p != 2 and q != 2
        )
    )
    return (grad_x, grad_y, hess_xx, hess_yy, hess_xy)


def sample(field, weights_x, weights_y, nrows, ncols):
    total = jnp.zeros((nrows // TILE_R, TILE_R, ncols // TILE_C, TILE_C), jnp.float32)
    for brow in range(4):
        inner = jnp.zeros_like(total)
        for acol in range(4):
            piece = field[brow : brow + nrows, acol : acol + ncols]
            piece = piece.reshape(nrows // TILE_R, TILE_R, ncols // TILE_C, TILE_C)
            inner = inner + weights_x[acol] * piece
        total = total + weights_y[brow] * inner
    return total.reshape(nrows, ncols)


def advance(state, tile, weights_x, weights_y, lens):
    nrows = tile.shape[0] - 8
    ncols = tile.shape[1] - 8
    fields = derivatives(tile.astype(jnp.float32))
    grad_x, grad_y, hess_xx, hess_yy, hess_xy = [
        sample(f, weights_x, weights_y, nrows, ncols) for f in fields
    ]
    shift_x, shift_y, a_11, a_12, a_21, a_22 = state
    shift_x = shift_x + lens * grad_x
    shift_y = shift_y + lens * grad_y
    new_11 = a_11 - lens * (hess_xx * a_11 + hess_xy * a_21)
    new_12 = a_12 - lens * (hess_xx * a_12 + hess_xy * a_22)
    new_21 = a_21 - lens * (hess_xy * a_11 + hess_yy * a_21)
    new_22 = a_22 - lens * (hess_xy * a_12 + hess_yy * a_22)
    return (shift_x, shift_y, new_11, new_12, new_21, new_22)


def cut_columns(band, shift, flip, width):
    flipped = jnp.where(flip == 1, band[..., ::-1], band)
    extended = jnp.concatenate([flipped, flipped[..., : width + 8]], axis=-1)
    start = (shift - 4) % band.shape[-1]
    return lax.dynamic_slice_in_dim(extended, start, width + 8, flipped.ndim - 1)


def add_edges(blocks):
    return extended_2(blocks, (("sky", 1),), 4)


def body(potential_stock, plane_pick, col_shift, mirror, subcell, lens_weight):
    nrows = subcell.shape[0] * TILE_R
    ncols = subcell.shape[1] * TILE_C
    held = potential_stock.shape[0]
    weights_x, weights_y = tap_weights(subcell)
    zeros = jnp.zeros((nrows, ncols), jnp.float32)
    ones = jnp.ones((nrows, ncols), jnp.float32)
    state = (zeros, zeros, ones, zeros, zeros, ones)
    for plane in range(PLANES):
        entry = plane_pick[plane]
        own = lax.dynamic_index_in_dim(potential_stock, entry % held, 0, keepdims=False)
        band = spread(own, "real", entry // held)
        view = add_edges(cut_columns(band, col_shift[0, plane], mirror[0, plane], ncols)[None])[0]
        state = advance(state, view, weights_x, weights_y, lens_weight[plane])
    deflect = jnp.stack([state[0], state[1]])[:, None]
    distort = jnp.stack([state[2], state[3], state[4], state[5]])[:, None]
    return (deflect, distort)


def solution(mesh):
    return jax.shard_map(
        body,
        mesh=mesh,
        in_specs=(
            P("real", "sky", None),
            P(),
            P("real", None),
            P("real", None),
            P("sky", None),
            P(),
        ),
        out_specs=(P(None, "real", "sky", None), P(None, "real", "sky", None)),
        check_vma=False,
    )
```

profile of v0, /device:TPU:0, one launch (start us, length us, event | category | flops | bytes accessed | tf_op | source)
XLA Modules:
  0.0 334.8 jit_solution(15241077179185360147)
XLA Ops:
  7.2 0.0 all-reduce.3.cloned.1.call-start
  7.2 1.4 fusion.436
  18.8 4.3 %select_bitcast_fusion.3 = (bf16[32,16384]{1,0:T(8,128)(2,1)}, bf16[32,16384]{1,0:T(8,128)(2,1)}, bf16[32,16384]{1,0:T(8,128)(2,1)}, bf16[32,16384]{1,0:T(8,128)(2,1)}) fusion(bf16[2,32,16384]{2,1,0:T(8,128)(2,1)} %param.6, s32[]{:T(128)S(6)} %select_n.154, pred[]{:T(512)S(6)} %eq.49, s32[]{:T(128)S(6)} %select_n.164, pred[]{:T(512)S(6)} %eq.52, ...), kind=kLoop, calls=%fused_computation.412 | loop fusion | flops 2097152 | bytes 8388628 | tf_op jit(solution)/shard_map/jit(_where)/select_n | solution.py:30
  23.0 0.0 copy-start.7
  23.0 0.0 all-reduce.3.cloned.1.call-update
  23.1 0.6 copy-done.4
  23.7 0.7 fusion.435
  27.0 0.0 copy-done.5
  27.0 0.7 fusion.434
  30.2 0.0 copy-done.6
  30.2 0.7 fusion.433
  30.9 80.6 %all-reduce.3.cloned.1.call-done = (bf16[32,16384]{1,0:T(8,128)(2,1)}, bf16[32,16384]{1,0:T(8,128)(2,1)}, bf16[32,16384]{1,0:T(8,128)(2,1)}, bf16[32,16384]{1,0:T(8,128)(2,1)}) async-done(((bf16[32,16384]{1,0:T(8,128)(2,1)}, bf16[32,16384]{1,0:T(8,128)(2,1)}, bf16[32,16384]{1,0:T(8,128)(2,1)}, bf16[32,16384]{1,0:T(8,128)(2,1)}), (bf16[32,16384]{1,0:T(8,128)(2,1)}, bf16[32,16384]{1,0:T(8,128)(2,1)}, ...) | async-done | bytes 4194320 | tf_op jit(solution)/shard_map/psum | solution.py:31
  111.5 50.0 %rev.15 = bf16[32,16384]{1,0:T(8,128)(2,1)S(1)} reverse(bf16[32,16384]{1,0:T(8,128)(2,1)} %get-tuple-element.2), dimensions={1} | reverse | bytes 2097152 | tf_op jit(solution)/shard_map/rev | solution.py:105
  161.5 43.2 %rev.14 = bf16[32,16384]{1,0:T(8,128)(2,1)} reverse(bf16[32,16384]{1,0:T(8,128)(2,1)S(1)} %copy-done.3), dimensions={1} | reverse | bytes 2097152 | tf_op jit(solution)/shard_map/rev | solution.py:105
  204.8 1.4 broadcast_select_fusion
  206.2 0.2 fusion.387
  206.5 0.6 fusion.432
  207.1 4.2 %collective-permute-start.7 = (bf16[1,4,2056]{2,1,0:T(4,128)(2,1)}, bf16[1,4,2056]{2,1,0:T(4,128)(2,1)S(1)}, u32[]{:S(2)}, u32[]{:S(2)}) collective-permute-start(bf16[1,4,2056]{2,1,0:T(4,128)(2,1)} %get-tuple-element.60), channel_id=1, source_target_pairs={{1,0},{2,1},{3,2},{4,3},{5,4},{6,5},{7,6},{0,7},{9,8},{10,9},{11,1... | collective-permute-start | bytes 49352 | tf_op jit(solution)/shard_map/ppermute | solution.py:24
  211.3 0.0 collective-permute-start.6
  211.3 0.2 fusion.386
  211.6 0.0 copy-start.1
  211.6 0.6 fusion.431
  212.2 4.7 %collective-permute-start.5 = (bf16[1,4,2056]{2,1,0:T(4,128)(2,1)}, bf16[1,4,2056]{2,1,0:T(4,128)(2,1)S(1)}, u32[]{:S(2)}, u32[]{:S(2)}) collective-permute-start(bf16[1,4,2056]{2,1,0:T(4,128)(2,1)} %get-tuple-element.58), channel_id=1, source_target_pairs={{1,0},{2,1},{3,2},{4,3},{5,4},{6,5},{7,6},{0,7},{9,8},{10,9},{11,1... | collective-permute-start | bytes 49352 | tf_op jit(solution)/shard_map/ppermute | solution.py:24
  216.9 10.6 %rev.13 = bf16[32,16384]{1,0:T(8,128)(2,1)S(1)} reverse(bf16[32,16384]{1,0:T(8,128)(2,1)S(1)} %copy-done), dimensions={1} | reverse | bytes 2097152 | tf_op jit(solution)/shard_map/rev | solution.py:105
  227.6 43.2 %rev.12 = bf16[32,16384]{1,0:T(8,128)(2,1)} reverse(bf16[32,16384]{1,0:T(8,128)(2,1)S(1)} %copy-done.1), dimensions={1} | reverse | bytes 2097152 | tf_op jit(solution)/shard_map/rev | solution.py:105
  270.8 0.2 broadcast_select_fusion.2
  271.0 0.2 fusion.384
  271.3 0.1 collective-permute-start.1
  271.4 2.0 collective-permute-start
  273.4 0.2 fusion.385
  273.6 1.5 collective-permute-done.1
  275.1 2.7 collective-permute-start.3
  277.8 0.1 collective-permute-done
  277.9 0.0 collective-permute-start.2
  277.9 0.1 fusion.376
  277.9 0.9 add_add_fusion.7
  278.8 1.5 fusion.45
  280.3 0.0 collective-permute-done.3
  280.3 0.4 collective-permute-start.4
  280.7 3.6 %collective-permute-done.2 = bf16[1,4,2056]{2,1,0:T(4,128)(2,1)S(1)} collective-permute-done((bf16[1,4,2056]{2,1,0:T(4,128)(2,1)S(1)}, bf16[1,4,2056]{2,1,0:T(4,128)(2,1)S(1)}, u32[]{:S(2)}, u32[]{:S(2)}) %collective-permute-start.2) | collective-permute-done | bytes 16480 | tf_op jit(solution)/shard_map/ppermute | solution.py:23
  284.3 0.1 fusion.377
  284.4 0.9 add_add_fusion.3
  285.3 1.5 fusion.30
  286.8 0.0 collective-permute-done.7
  286.8 0.0 collective-permute-done.6
  286.8 0.1 fusion.379
  286.8 0.9 add_add_fusion
  287.7 1.5 fusion
  289.2 0.0 collective-permute-done.5
  289.2 0.0 collective-permute-done.4
  289.3 0.1 fusion.378
  289.3 0.9 add_add_fusion.1
  290.2 1.5 fusion.15
  291.7 6.8 %fusion.87 = f32[1,32,2048]{2,1,0:T(8,128)S(1)} fusion(f32[35,2051]{1,0:T(8,128)S(1)} %get-tuple-element.38, f32[35,2051]{1,0:T(8,128)S(1)} %get-tuple-element.42, f32[35,2051]{1,0:T(8,128)S(1)} %get-tuple-element.46, f32[35,2051]{1,0:T(8,128)S(1)} %get-tuple-element.50, f32[]{:T(128)} %bitcast.32, f32[]{:T(128)} %bitcast.24, f32[]{:T(128)} %bitcast.16, ...), kind=kLoop, calls=%fused_computation.597 | loop fusion | flops 9633792 | bytes 17041424 | tf_op jit(solution)/shard_map/stack | solution.py:129
  298.5 6.6 %fusion.67 = f32[1,32,2048]{2,1,0:T(8,128)S(1)} fusion(f32[35,2051]{1,0:T(8,128)S(1)} %get-tuple-element.39, f32[35,2051]{1,0:T(8,128)S(1)} %get-tuple-element.43, f32[35,2051]{1,0:T(8,128)S(1)} %get-tuple-element.47, f32[35,2051]{1,0:T(8,128)S(1)} %get-tuple-element.51, f32[]{:T(128)} %bitcast.32, f32[]{:T(128)} %bitcast.24, f32[]{:T(128)} %bitcast.16, ...), kind=kLoop, calls=%fused_computation.577 | loop fusion | flops 9633792 | bytes 17041424 | tf_op jit(solution)/shard_map/stack | solution.py:129
  305.1 0.8 maximum_bitcast_fusion.1
  306.0 6.1 %multiply_subtract_fusion.9 = (f32[32,2048]{1,0:T(8,128)S(1)}, f32[32,2048]{1,0:T(8,128)S(1)}, f32[32,2048]{1,0:T(8,128)S(1)}, f32[32,2048]{1,0:T(8,128)S(1)}, f...) fusion(f32[]{:T(128)} %bitcast.16, f32[]{:T(128)} %bitcast, f32[35,2051]{1,0:T(8,128)S(1)} %get-tuple-element.48, ...), kind=kLoop, calls=%fused_computation.899 | loop fusion | flops 12320768 | bytes 22546440 | tf_op jit(solution)/shard_map/sub | solution.py:97
  312.0 2.8 multiply_subtract_fusion.8
  314.9 1.4 multiply_subtract_fusion.2
  316.3 6.2 %subtract_bitcast_fusion.3 = (f32[1,32,2048]{2,1,0:T(8,128)S(1)}, f32[32,2048]{1,0:T(8,128)S(1)}, f32[32,2048]{1,0:T(8,128)S(1)}, f32[32,2048]{1,0:T(8,128)S(1)}...) fusion(f32[]{:T(128)} %bitcast.32, ...), kind=kLoop, calls=%fused_computation.895 | loop fusion | flops 12451840 | bytes 23595016 | tf_op jit(solution)/shard_map/stack | solution.py:130
  322.5 2.2 subtract_bitcast_fusion.1
  324.7 1.5 subtract_bitcast_fusion.2
  326.2 0.7 subtract_bitcast_fusion
  326.9 1.1 maximum_bitcast_fusion
  (19 shorter events, 0.1 us)
Async XLA Ops:
  7.2 104.3 %all-reduce.3.cloned.1.call-start = ((), (), s32[]{:S(2)}) async-start(), calls=%async_computation | async-start | bytes 8388608 | tf_op jit(solution)/shard_map/psum | solution.py:31
  23.0 0.7 copy-start.4
  23.0 4.0 %copy-start.5 = (s32[1,4]{1,0:T(1,128)S(1)}, s32[1,4]{1,0:T(1,128)}, u32[]{:S(2)}) copy-start(s32[1,4]{1,0:T(1,128)} %param.9) | copy-start | bytes 52
  23.0 7.2 %copy-start.6 = (f32[4]{0:T(128)S(1)}, f32[4]{0:T(128)}, u32[]{:S(2)}) copy-start(f32[4]{0:T(128)} %param.11) | copy-start | bytes 52
  23.0 7.9 %copy-start.7 = (s32[4,16]{1,0:T(4,128)S(1)}, s32[4,16]{1,0:T(4,128)}, u32[]{:S(2)}) copy-start(s32[4,16]{1,0:T(4,128)} %param.10) | copy-start | bytes 772
  111.5 50.0 %copy-start.3 = (bf16[32,16384]{1,0:T(8,128)(2,1)S(1)}, bf16[32,16384]{1,0:T(8,128)(2,1)}, u32[]{:S(2)}) copy-start(bf16[32,16384]{1,0:T(8,128)(2,1)} %get-tuple-element.3) | copy-start | bytes 3145732
  161.5 43.2 %copy-start.2 = (bf16[32,16384]{1,0:T(8,128)(2,1)S(1)}, bf16[32,16384]{1,0:T(8,128)(2,1)}, u32[]{:S(2)}) copy-start(bf16[32,16384]{1,0:T(8,128)(2,1)} %get-tuple-element.2) | copy-start | bytes 3145732
  206.4 10.5 %copy-start = (bf16[32,16384]{1,0:T(8,128)(2,1)S(1)}, bf16[32,16384]{1,0:T(8,128)(2,1)}, u32[]{:S(2)}) copy-start(bf16[32,16384]{1,0:T(8,128)(2,1)} %get-tuple-element.4) | copy-start | bytes 3145732
  207.1 79.7 %collective-permute-start.7 = (bf16[1,4,2056]{2,1,0:T(4,128)(2,1)}, bf16[1,4,2056]{2,1,0:T(4,128)(2,1)S(1)}, u32[]{:S(2)}, u32[]{:S(2)}) collective-permute-start(bf16[1,4,2056]{2,1,0:T(4,128)(2,1)} %get-tuple-element.60), channel_id=1, source_target_pairs={{1,0},{2,1},{3,2},{4,3},{5,4},{6,5},{7,6},{0,7},{9,8},{10,9},{11,1... | collective-permute-start | bytes 49352 | tf_op jit(solution)/shard_map/ppermute | solution.py:24
  211.3 75.5 %collective-permute-start.6 = (bf16[1,4,2056]{2,1,0:T(4,128)(2,1)}, bf16[1,4,2056]{2,1,0:T(4,128)(2,1)S(1)}, u32[]{:S(2)}, u32[]{:S(2)}) collective-permute-start(bf16[1,4,2056]{2,1,0:T(4,128)(2,1)} %get-tuple-element.59), channel_id=1, source_target_pairs={{0,1},{1,2},{2,3},{3,4},{4,5},{5,6},{6,7},{7,0},{8,9},{9,10},{10,1... | collective-permute-start | bytes 49352 | tf_op jit(solution)/shard_map/ppermute | solution.py:23
  211.6 16.0 %copy-start.1 = (bf16[32,16384]{1,0:T(8,128)(2,1)S(1)}, bf16[32,16384]{1,0:T(8,128)(2,1)}, u32[]{:S(2)}) copy-start(bf16[32,16384]{1,0:T(8,128)(2,1)} %get-tuple-element.5) | copy-start | bytes 3145732
  212.2 77.0 %collective-permute-start.5 = (bf16[1,4,2056]{2,1,0:T(4,128)(2,1)}, bf16[1,4,2056]{2,1,0:T(4,128)(2,1)S(1)}, u32[]{:S(2)}, u32[]{:S(2)}) collective-permute-start(bf16[1,4,2056]{2,1,0:T(4,128)(2,1)} %get-tuple-element.58), channel_id=1, source_target_pairs={{1,0},{2,1},{3,2},{4,3},{5,4},{6,5},{7,6},{0,7},{9,8},{10,9},{11,1... | collective-permute-start | bytes 49352 | tf_op jit(solution)/shard_map/ppermute | solution.py:24
  271.3 3.8 %collective-permute-start.1 = (bf16[1,4,2056]{2,1,0:T(4,128)(2,1)S(1)}, bf16[1,4,2056]{2,1,0:T(4,128)(2,1)S(1)}, u32[]{:S(2)}, u32[]{:S(2)}) collective-permute-start(bf16[1,4,2056]{2,1,0:T(4,128)(2,1)S(1)} %get-tuple-element.54), channel_id=1, source_target_pairs={{1,0},{2,1},{3,2},{4,3},{5,4},{6,5},{7,6},{0,7},{9,8},{10,9},{11,1... | collective-permute-start | bytes 49352 | tf_op jit(solution)/shard_map/ppermute | solution.py:24
  271.4 6.5 %collective-permute-start = (bf16[1,4,2056]{2,1,0:T(4,128)(2,1)S(1)}, bf16[1,4,2056]{2,1,0:T(4,128)(2,1)S(1)}, u32[]{:S(2)}, u32[]{:S(2)}) collective-permute-start(bf16[1,4,2056]{2,1,0:T(4,128)(2,1)S(1)} %get-tuple-element.53), channel_id=1, source_target_pairs={{0,1},{1,2},{2,3},{3,4},{4,5},{5,6},{6,7},{7,0},{8,9},{9,10},{10,1... | collective-permute-start | bytes 49352 | tf_op jit(solution)/shard_map/ppermute | solution.py:23
  275.1 5.2 %collective-permute-start.3 = (bf16[1,4,2056]{2,1,0:T(4,128)(2,1)S(1)}, bf16[1,4,2056]{2,1,0:T(4,128)(2,1)S(1)}, u32[]{:S(2)}, u32[]{:S(2)}) collective-permute-start(bf16[1,4,2056]{2,1,0:T(4,128)(2,1)S(1)} %get-tuple-element.56), channel_id=1, source_target_pairs={{1,0},{2,1},{3,2},{4,3},{5,4},{6,5},{7,6},{0,7},{9,8},{10,9},{11,1... | collective-permute-start | bytes 49352 | tf_op jit(solution)/shard_map/ppermute | solution.py:24
  277.9 6.4 %collective-permute-start.2 = (bf16[1,4,2056]{2,1,0:T(4,128)(2,1)S(1)}, bf16[1,4,2056]{2,1,0:T(4,128)(2,1)S(1)}, u32[]{:S(2)}, u32[]{:S(2)}) collective-permute-start(bf16[1,4,2056]{2,1,0:T(4,128)(2,1)S(1)} %get-tuple-element.55), channel_id=1, source_target_pairs={{0,1},{1,2},{2,3},{3,4},{4,5},{5,6},{6,7},{7,0},{8,9},{9,10},{10,1... | collective-permute-start | bytes 49352 | tf_op jit(solution)/shard_map/ppermute | solution.py:23
  280.3 8.9 %collective-permute-start.4 = (bf16[1,4,2056]{2,1,0:T(4,128)(2,1)S(1)}, bf16[1,4,2056]{2,1,0:T(4,128)(2,1)S(1)}, u32[]{:S(2)}, u32[]{:S(2)}) collective-permute-start(bf16[1,4,2056]{2,1,0:T(4,128)(2,1)S(1)} %get-tuple-element.57), channel_id=1, source_target_pairs={{0,1},{1,2},{2,3},{3,4},{4,5},{5,6},{6,7},{7,0},{8,9},{9,10},{10,1... | collective-permute-start | bytes 49352 | tf_op jit(solution)/shard_map/ppermute | solution.py:23
Sparse Core Ops, SparseCore 0:
  23.2 88.2 all-reduce.2
where the time goes:
time: 338 us; the launch traced here: 335 us
  local copies, waits for them, and re-layouts  152 us (45%)
  waiting for transfers between devices  85.7 us (25%)
  other arithmetic  52.8 us (16%)
  between operations  29.7 us (9%)
  starting transfers between devices  14.2 us (4%)
    rev x4, local copies, waits for them, and re-layouts, cut_columns(): flipped = jnp.where(flip == 1, band[..., ::-1], band)  147 us
    psum x1, waiting for transfers between devices, spread(): return lax.psum(kept, axis)  80.6 us
    another operation x2, other arithmetic, body(): deflect = jnp.stack([state[0], state[1]])[:, None]  13.4 us
    ppermute x4, starting transfers between devices, extended_2(): after = lax.ppermute(first, axis, down)  11.7 us
    another operation x4, other arithmetic, body(): distort = jnp.stack([state[2], state[3], state[4], state[5]])[:, None]  10.6 us
  transfers between devices with their start and end apart: 9, of which 4 were waited for; matrix products, arithmetic and copies ran while one was open for 19% of the time, Pallas kernels for 0%

commit v1 on v0

v1 whole, which is shorter than its diff:
```python
import functools

import jax
import jax.numpy as jnp
from jax import lax
from jax.experimental import pallas as pl
from jax.experimental.pallas import tpu as pltpu
from jax.sharding import PartitionSpec as P

SUB = 4
TILE_R = 8
TILE_C = 128
EDGE = 4
MESH = pl.DeviceIdType.MESH

first_coef = (1.0 / 12.0, -8.0 / 12.0, 0.0, 8.0 / 12.0, -1.0 / 12.0)
second_coef = (-1.0 / 12.0, 16.0 / 12.0, -30.0 / 12.0, 16.0 / 12.0, -1.0 / 12.0)


def cubic(t):
    return (
        (-(t**3) + 2 * t**2 - t) / 2,
        (3 * t**3 - 5 * t**2 + 2) / 2,
        (-3 * t**3 + 4 * t**2 + t) / 2,
        (t**3 - t**2) / 2,
    )


def convolved(taps, coef):
    out = [0.0] * 8
    for a, w in enumerate(taps):
        for q, c in enumerate(coef):
            out[a + q] += w * c
    return out


def filter_table():
    rows = []
    for o in range(SUB):
        taps = cubic((o + 0.5) / SUB)
        rows.append(list(taps) + convolved(taps, first_coef) + convolved(taps, second_coef))
    return rows


TABLE = filter_table()
NTAB = 20


def exchange_kernel(
    stock_ref, pick_ref, shift_ref, mirror_ref,
    main_ref, before_ref, after_ref,
    stock_t, tiles, send, edge32, esend, shifts_v, mirrors_v, shifts, mirrors,
    meta_send, meta_recv, local_sem, stock_sem, main_send, main_recv, edge_send, edge_recv,
):
    held, rows, cols = stock_ref.shape
    ntiles = cols // TILE_C
    out_tiles = main_ref.shape[2] // rows
    planes = pick_ref.shape[0]
    peers = lax.axis_size("real")
    strips = lax.axis_size("sky")
    me = lax.axis_index("real")
    strip = lax.axis_index("sky")
    above = lax.rem(strip + strips - 1, strips)
    below = lax.rem(strip + 1, strips)

    for e in range(held):
        @pl.loop(0, ntiles)
        def _(t):
            at = pl.ds(pl.multiple_of(t * TILE_C, TILE_C), TILE_C)
            pltpu.make_async_copy(
                stock_ref.at[e, :, at], stock_t.at[e * ntiles + t], stock_sem).start()

    barrier = pltpu.get_barrier_semaphore()
    for off in range(peers):
        r = lax.rem(me + off, peers)
        for s in (strip, above, below):
            if off == 0 and s is strip:
                continue
            pl.semaphore_signal(barrier, inc=1, device_id=(r, s), device_id_type=MESH)
    pl.semaphore_wait(barrier, 3 * peers - 1)

    def meta_copies(off):
        to = lax.rem(me + off, peers)
        return [
            pltpu.make_async_remote_copy(
                src_ref=src, dst_ref=dst.at[me], send_sem=meta_send.at[q, off],
                recv_sem=meta_recv.at[q, off], device_id=(to, strip), device_id_type=MESH)
            for q, (src, dst) in enumerate(((shift_ref, shifts_v), (mirror_ref, mirrors_v)))
        ]

    for off in range(1, peers):
        for copy in meta_copies(off):
            copy.start()
    own = [pltpu.make_async_copy(src, dst.at[me], local_sem.at[q])
           for q, (src, dst) in enumerate(((shift_ref, shifts_v), (mirror_ref, mirrors_v)))]
    for copy in own:
        copy.start()
    for copy in own:
        copy.wait()
    for off in range(1, peers):
        for copy in meta_copies(off):
            copy.wait()
    down = [pltpu.make_async_copy(src, dst, local_sem.at[q])
            for q, (src, dst) in enumerate(((shifts_v, shifts), (mirrors_v, mirrors)))]
    for copy in down:
        copy.start()
    for copy in down:
        copy.wait()

    lane_in = lax.broadcasted_iota(jnp.int32, (2 * TILE_C, TILE_C), 0)
    lane_out = lax.broadcasted_iota(jnp.int32, (2 * TILE_C, TILE_C), 1)

    def main_copy(off):
        to = lax.rem(me + off, peers)
        return pltpu.make_async_remote_copy(
            src_ref=send.at[off], dst_ref=main_ref.at[me], send_sem=main_send.at[off],
            recv_sem=main_recv.at[off], device_id=(to, strip), device_id_type=MESH)

    def edge_copies(off):
        to = lax.rem(me + off, peers)
        return [
            pltpu.make_async_remote_copy(
                src_ref=esend.at[off, 0], dst_ref=after_ref.at[me], send_sem=edge_send.at[0, off],
                recv_sem=edge_recv.at[0, off], device_id=(to, above), device_id_type=MESH),
            pltpu.make_async_remote_copy(
                src_ref=esend.at[off, 1], dst_ref=before_ref.at[me], send_sem=edge_send.at[1, off],
                recv_sem=edge_recv.at[1, off], device_id=(to, below), device_id_type=MESH),
        ]

    def cut(off):
        to = lax.rem(me + off, peers)
        for e in range(held):
            q = me * held + e
            shift = jnp.int32(0)
            turned = jnp.int32(0)
            for k in range(planes):
                hit = pick_ref[k] == q
                shift = jnp.where(hit, shifts[to, 0, k], shift)
                turned = jnp.where(hit, mirrors[to, 0, k], turned)
            step = 1 - 2 * turned
            start = turned * (cols + EDGE - 1 - shift) + (1 - turned) * (shift + cols - EDGE)
            start = lax.rem(start, cols)
            base = lax.div(start, TILE_C)
            inner = start - base * TILE_C
            for u in range(out_tiles + 1):
                at = e * ntiles + lax.rem(base + step * u + ntiles, ntiles)
                tiles[u * rows:(u + 1) * rows, :] = stock_t[at]
            near = lane_in == inner + step * lane_out
            far = lane_in - TILE_C == inner + step * (lane_out - TILE_C)
            choose = ((near & (lane_in < TILE_C)) | (far & (lane_in >= TILE_C)))
            choose = choose.astype(jnp.float32).astype(jnp.bfloat16)
            n = out_tiles * rows
            pairs = jnp.concatenate([tiles[0:n, :], tiles[rows:n + rows, :]], axis=1)
            view = jnp.dot(pairs, choose, preferred_element_type=jnp.float32)
            send[off, e] = view.astype(jnp.bfloat16)
            for t in range(out_tiles):
                edge32[0, t * EDGE:(t + 1) * EDGE, :] = view[t * rows:t * rows + EDGE, :]
                edge32[1, t * EDGE:(t + 1) * EDGE, :] = view[(t + 1) * rows - EDGE:(t + 1) * rows, :]
            esend[off, 0, e] = edge32[0].astype(jnp.bfloat16)
            esend[off, 1, e] = edge32[1].astype(jnp.bfloat16)

    pltpu.make_async_copy(stock_t, stock_t, stock_sem).wait()
    edge32[...] = jnp.zeros_like(edge32)
    order = sorted(range(1, peers), key=lambda off: abs(2 * off - peers)) + [0]
    for off in order:
        cut(off)
        if off:
            main_copy(off).start()
        else:
            keep = pltpu.make_async_copy(send.at[0], main_ref.at[me], local_sem.at[0])
            keep.start()
        for copy in edge_copies(off):
            copy.start()
    keep.wait()
    for off in order:
        if off:
            main_copy(off).wait()
        for copy in edge_copies(off):
            copy.wait()


def trace_kernel(
    pick_ref, subcell_ref, lens_ref, main_ref, before_ref, after_ref,
    deflect_ref, distort_ref,
    main_v, before_v, after_v, view, table, sems,
):
    planes = pick_ref.shape[0]
    held = main_ref.shape[1]
    nrows = deflect_ref.shape[2]
    ncols = deflect_ref.shape[3]
    out_tiles = main_v.shape[1] // nrows

    copies = []
    for k in range(planes):
        group = pick_ref[k] // held
        e = lax.rem(pick_ref[k], held)
        copies.append([
            pltpu.make_async_copy(src.at[group, e], dst.at[k], sems.at[k, q])
            for q, (src, dst) in enumerate(
                ((main_ref, main_v), (before_ref, before_v), (after_ref, after_v)))
        ])
        for copy in copies[k]:
            copy.start()
    for o in range(SUB):
        for m in range(NTAB):
            table[o, m] = jnp.float32(TABLE[o][m])
    for k in range(planes):
        for copy in copies[k]:
            copy.wait()
        up = before_v[k].astype(jnp.float32)
        down = after_v[k].astype(jnp.float32)
        for t in range(out_tiles):
            view[k, t, TILE_R:TILE_R + nrows, :] = main_v[k, t * nrows:(t + 1) * nrows, :].astype(jnp.float32)
            view[k, t, TILE_R - EDGE:TILE_R, :] = up[t * EDGE:(t + 1) * EDGE]
            view[k, t, TILE_R + nrows:TILE_R + nrows + EDGE, :] = down[t * EDGE:(t + 1) * EDGE]

    def tile(i, j):
        o = subcell_ref[i, j]
        oy = o // SUB
        ox = o - oy * SUB
        wx = [table[ox, m] for m in range(NTAB)]
        wy = [table[oy, m] for m in range(NTAB)]
        x0, x1, x2 = wx[:4], wx[4:12], wx[12:20]
        y0, y1, y2 = wy[:4], wy[4:12], wy[12:20]
        shape = (TILE_R, TILE_C)
        zero = jnp.zeros(shape, jnp.float32)
        one = jnp.ones(shape, jnp.float32)
        dx, dy, a11, a12, a21, a22 = zero, zero, one, zero, zero, one
        for k in range(planes):
            parts = []
            for side in range(2):
                v = [view[k, j + side, pl.ds(TILE_R + i * TILE_R + n, TILE_R), :] for n in range(-3, 5)]
                parts.append((
                    sum(y0[b] * v[b + 2] for b in range(4)),
                    sum(y1[b] * v[b] for b in range(8)),
                    sum(y2[b] * v[b] for b in range(8)),
                ))
            f0, f1, f2 = [jnp.concatenate([parts[0][q], parts[1][q]], axis=1) for q in range(3)]
            s0 = [f0[:, m + 1:m + 1 + TILE_C] for m in range(8)]
            s1 = [f1[:, m + 1:m + 1 + TILE_C] for m in range(8)]
            s2 = [f2[:, m + 3:m + 3 + TILE_C] for m in range(4)]
            gx = sum(x1[m] * s0[m] for m in range(8))
            xx = sum(x2[m] * s0[m] for m in range(8))
            xy = sum(x1[m] * s1[m] for m in range(8))
            gy = sum(x0[m] * s1[m + 2] for m in range(4))
            yy = sum(x0[m] * s2[m] for m in range(4))
            lens = lens_ref[k]
            dx = dx + lens * gx
            dy = dy + lens * gy
            xx, xy, yy = lens * xx, lens * xy, lens * yy
            a11, a12, a21, a22 = (
                a11 - (xx * a11 + xy * a21),
                a12 - (xx * a12 + xy * a22),
                a21 - (xy * a11 + yy * a21),
                a22 - (xy * a12 + yy * a22),
            )
        at = pl.ds(pl.multiple_of(j * TILE_C, TILE_C), TILE_C)
        rs = slice(i * TILE_R, (i + 1) * TILE_R)
        deflect_ref[0, 0, rs, at] = dx
        deflect_ref[1, 0, rs, at] = dy
        for n, a in enumerate((a11, a12, a21, a22)):
            distort_ref[n, 0, rs, at] = a

    @pl.loop(0, ncols // TILE_C)
    def _(j):
        for i in range(nrows // TILE_R):
            tile(i, j)


def body(potential_stock, plane_pick, col_shift, mirror, subcell, lens_weight):
    held, rows, cols = potential_stock.shape
    peers = lax.axis_size("real")
    planes = plane_pick.shape[0]
    ncols = subcell.shape[1] * TILE_C
    out_tiles = -(-(ncols + 2 * EDGE) // TILE_C)
    erows = -(-(out_tiles * EDGE) // 16) * 16
    n = out_tiles * rows
    vm = pl.BlockSpec(memory_space=pltpu.VMEM)
    sm = pl.BlockSpec(memory_space=pltpu.SMEM)
    anyw = pl.BlockSpec(memory_space=pl.ANY)
    bf = jnp.bfloat16
    dma = pltpu.SemaphoreType.DMA
    main, before, after = pl.pallas_call(
        exchange_kernel,
        out_shape=(
            jax.ShapeDtypeStruct((peers, held, n, TILE_C), bf),
            jax.ShapeDtypeStruct((peers, held, erows, TILE_C), bf),
            jax.ShapeDtypeStruct((peers, held, erows, TILE_C), bf),
        ),
        in_specs=[anyw, sm, vm, vm],
        out_specs=(anyw, anyw, anyw),
        scratch_shapes=[
            pltpu.VMEM((held * (cols // TILE_C), rows, TILE_C), bf),
            pltpu.VMEM((n + rows, TILE_C), bf),
            pltpu.VMEM((peers, held, n, TILE_C), bf),
            pltpu.VMEM((2, erows, TILE_C), jnp.float32),
            pltpu.VMEM((peers, 2, held, erows, TILE_C), bf),
            pltpu.VMEM((peers, 1, planes), jnp.int32),
            pltpu.VMEM((peers, 1, planes), jnp.int32),
            pltpu.SMEM((peers, 1, planes), jnp.int32),
            pltpu.SMEM((peers, 1, planes), jnp.int32),
            dma((2, peers)), dma((2, peers)), dma((2,)), dma,
            dma((peers,)), dma((peers,)), dma((2, peers)), dma((2, peers)),
        ],
        compiler_params=pltpu.CompilerParams(collective_id=0, has_side_effects=True),
        name="exchange",
    )(potential_stock, plane_pick, col_shift, mirror)
    f32 = jnp.float32
    nrows = subcell.shape[0] * TILE_R
    return pl.pallas_call(
        trace_kernel,
        out_shape=(
            jax.ShapeDtypeStruct((2, 1, nrows, ncols), f32),
            jax.ShapeDtypeStruct((4, 1, nrows, ncols), f32),
        ),
        in_specs=[sm, sm, sm, anyw, anyw, anyw],
        out_specs=(vm, vm),
        scratch_shapes=[
            pltpu.VMEM((planes, n, TILE_C), bf),
            pltpu.VMEM((planes, erows, TILE_C), bf),
            pltpu.VMEM((planes, erows, TILE_C), bf),
            pltpu.VMEM((planes, out_tiles, nrows + 2 * TILE_R, TILE_C), f32),
            pltpu.SMEM((SUB, NTAB), f32),
            dma((planes, 3)),
        ],
        name="trace",
    )(plane_pick, subcell, lens_weight, main, before, after)


def solution(mesh):
    return jax.shard_map(
        body,
        mesh=mesh,
        in_specs=(
            P("real", "sky", None),
            P(),
            P("real", None),
            P("real", None),
            P("sky", None),
            P(),
        ),
        out_specs=(P(None, "real", "sky", None), P(None, "real", "sky", None)),
        check_vma=False,
    )
```

time: 338 us -> 73 us (0.22)
  local copies, waits for them, and re-layouts: 152 us -> 0 us
  waiting for transfers between devices: 85.7 us -> 0 us
  Pallas kernels: 0 us -> 72.2 us
  other arithmetic: 52.8 us -> 0 us
  between operations: 29.7 us -> 0.64 us
  starting transfers between devices: 14.2 us -> 0 us
    rev x4 -> x0, local copies, waits for them, and re-layouts: 147 us -> none  [cut_columns(): flipped = jnp.where(flip == 1, band[..., ::-1], band)]
    psum x1 -> x0, waiting for transfers between devices: 80.6 us -> none  [spread(): return lax.psum(kept, axis)]
    pallas_call x0 -> x2, Pallas kernels: none -> 72.2 us  [the longest x1 42.3 us: body(): pl.pallas_call(trace_kernel, out_shape=(jax.ShapeDtypeStruct((2, 1, nrows...]
    another operation x6 -> x0, other arithmetic: 24 us -> none  [the longest x2 13.4 us: body(): deflect = jnp.stack([state[0], state[1]])[:, None]]
    ppermute x8 -> x0, starting transfers between devices: 14.1 us -> none  [the longest x4 11.7 us: extended_2(): after = lax.ppermute(first, axis, down)]
    sub x3 -> x0, other arithmetic: 10.3 us -> none  [the longest x1 6.07 us: advance(): new_11 = a_11 - lens * (hess_xx * a_11 + hess_xy * a_21)]
    add x8 -> x0, other arithmetic: 9.5 us -> none  [the longest x4 6 us: derivatives(): sum((first_coef[p] * first_coef[q] * window(p - 2, q - 2) for p in range(...]
    select_n x3 -> x0, other arithmetic: 5.9 us -> none  [the longest x1 4.26 us: spread(): jnp.where(lax.axis_index(axis) == source, value, 0).astype(value.dtype)]
  transfers between devices with their start and end apart: 9 -> 0, of which waited for: 4 -> 0; matrix products, arithmetic and copies ran while one was open for 19% -> 0% of each run, Pallas kernels for 0% -> 0%
where the time goes in v1:
time: 73 us; the launch traced here: 72.8 us
  Pallas kernels  72.2 us (99%)
    pallas_call x1, Pallas kernels, body(): pl.pallas_call(trace_kernel, out_shape=(jax.ShapeDtypeStruct((2, 1, nrows...  42.3 us
    pallas_call x1, Pallas kernels, body(): pl.pallas_call(exchange_kernel, out_shape=(jax.ShapeDtypeStruct((peers, h...  29.9 us

profile of v1, /device:TPU:0, one launch (start us, length us, event | category | flops | bytes accessed | tf_op | source)
XLA Modules:
  0.0 72.8 jit_solution(10714331522479689137)
XLA Ops:
  0.6 29.9 %exchange.1 = (bf16[4,2,544,128]{3,2,1,0:T(8,128)(2,1)}, bf16[4,2,80,128]{3,2,1,0:T(8,128)(2,1)}, bf16[4,2,80,128]{3,2,1,0:T(8,128)(2,1)}) custom-call(bf16[2,32,16384]{2,1,0:T(8,128)(2,1)} %stock_ref.1, s32[4]{0:T(128)} %pick_ref.3, s32[1,4]{1,0:T(1,128)} %shift_ref.1, s32[1,4]{1,0:T(1,128)} %mirror_ref.1), custom_call_target="tpu_custom_call" | custom-call | tf_op jit(solution)/shard_map/exchange/pallas_call | solution.py:283
  30.5 42.3 %trace.1 = (f32[2,1,32,2048]{3,2,1,0:T(8,128)}, f32[4,1,32,2048]{3,2,1,0:T(8,128)}) custom-call(s32[4]{0:T(128)} %pick_ref.3, s32[4,16]{1,0:T(4,128)} %subcell_ref.1, f32[4]{0:T(128)} %lens_ref.1, bf16[4,2,544,128]{3,2,1,0:T(8,128)(2,1)} %get-tuple-element.5.main_ref, bf16[4,2,80,128]{3,2,1,0:T(8,128)(2,1)} %get-tuple-element.6.before_ref, ...), custom_call_target="tpu_custom_call" | custom-call | tf_op jit(solution)/shard_map/trace/pallas_call | solution.py:310

commit v2 on v1

--- a/solution.py
+++ b/solution.py
@@ -1,7 +1,6 @@
-import functools
-
 import jax
 import jax.numpy as jnp
+import numpy as np
 from jax import lax
 from jax.experimental import pallas as pl
 from jax.experimental.pallas import tpu as pltpu
@@ -44,6 +43,22 @@
 
 TABLE = filter_table()
 NTAB = 20
+X_SCALE = 12288.0
+
+
+def column_filters():
+    full = np.zeros((2 * TILE_C, SUB, 3, TILE_C))
+    out = np.arange(TILE_C)
+    for o, row in enumerate(TABLE):
+        for m in range(4):
+            full[out + 3 + m, o, 0, out] = row[m] * X_SCALE
+        for m in range(8):
+            full[out + 1 + m, o, 1, out] = row[4 + m] * X_SCALE
+            full[out + 1 + m, o, 2, out] = row[12 + m] * X_SCALE
+    full = np.rint(full.reshape(2 * TILE_C, SUB * 3 * TILE_C)).astype(np.float32)
+    high = full.astype(jnp.bfloat16)
+    low = (full - high.astype(np.float32)).astype(jnp.bfloat16)
+    return np.concatenate([high, low], axis=0)
 
 
 def exchange_kernel(
@@ -180,16 +195,19 @@
 
 
 def trace_kernel(
-    pick_ref, subcell_ref, lens_ref, main_ref, before_ref, after_ref,
+    pick_ref, subcell_ref, lens_ref, filt_ref, main_ref, before_ref, after_ref,
     deflect_ref, distort_ref,
-    main_v, before_v, after_v, view, table, sems,
+    main_v, before_v, after_v, filt_v, edges, field, table, sems, filt_sem,
 ):
     planes = pick_ref.shape[0]
     held = main_ref.shape[1]
     nrows = deflect_ref.shape[2]
     ncols = deflect_ref.shape[3]
-    out_tiles = main_v.shape[1] // nrows
-
+    tiles = ncols // TILE_C
+    nfilt = filt_ref.shape[1] // TILE_C
+
+    filt_copy = pltpu.make_async_copy(filt_ref, filt_v, filt_sem)
+    filt_copy.start()
     copies = []
     for k in range(planes):
         group = pick_ref[k] // held
@@ -203,47 +221,58 @@
             copy.start()
     for o in range(SUB):
         for m in range(NTAB):
-            table[o, m] = jnp.float32(TABLE[o][m])
+            table[o, m] = jnp.float32(TABLE[o][m] / X_SCALE)
     for k in range(planes):
         for copy in copies[k]:
             copy.wait()
+    for k in range(planes):
         up = before_v[k].astype(jnp.float32)
         down = after_v[k].astype(jnp.float32)
-        for t in range(out_tiles):
-            view[k, t, TILE_R:TILE_R + nrows, :] = main_v[k, t * nrows:(t + 1) * nrows, :].astype(jnp.float32)
-            view[k, t, TILE_R - EDGE:TILE_R, :] = up[t * EDGE:(t + 1) * EDGE]
-            view[k, t, TILE_R + nrows:TILE_R + nrows + EDGE, :] = down[t * EDGE:(t + 1) * EDGE]
+        for t in range(tiles + 1):
+            edges[k, t, EDGE:2 * EDGE, :] = up[t * EDGE:(t + 1) * EDGE]
+            edges[k, t, 0:EDGE, :] = down[t * EDGE:(t + 1) * EDGE]
+    filt_copy.wait()
+
+    @pl.loop(0, planes)
+    def _(k):
+        m = tiles * nrows
+        flank = edges[k]
+        near = jnp.concatenate(
+            [main_v[k, 0:m, :], flank[0:tiles].reshape(tiles * TILE_R, TILE_C).astype(jnp.bfloat16)], axis=0)
+        far = jnp.concatenate(
+            [main_v[k, nrows:m + nrows, :], flank[1:tiles + 1].reshape(tiles * TILE_R, TILE_C).astype(jnp.bfloat16)],
+            axis=0)
+        lhs = jnp.concatenate([near, far, near, far], axis=1)
+        for c in range(0, nfilt, 2):
+            got = jnp.dot(lhs, filt_v[:, c * TILE_C:(c + 2) * TILE_C], preferred_element_type=jnp.float32)
+            for h in range(2):
+                part = got[:, h * TILE_C:(h + 1) * TILE_C]
+                ends = part[m:].reshape(tiles, TILE_R, TILE_C)
+                field[c + h, k, :, TILE_R:TILE_R + nrows, :] = part[:m].reshape(tiles, nrows, TILE_C)
+                field[c + h, k, :, 0:TILE_R, :] = ends
+                field[c + h, k, :, TILE_R + nrows:2 * TILE_R + nrows, :] = ends
 
     def tile(i, j):
         o = subcell_ref[i, j]
         oy = o // SUB
-        ox = o - oy * SUB
-        wx = [table[ox, m] for m in range(NTAB)]
+        fx = (o - oy * SUB) * 3
         wy = [table[oy, m] for m in range(NTAB)]
-        x0, x1, x2 = wx[:4], wx[4:12], wx[12:20]
         y0, y1, y2 = wy[:4], wy[4:12], wy[12:20]
         shape = (TILE_R, TILE_C)
         zero = jnp.zeros(shape, jnp.float32)
         one = jnp.ones(shape, jnp.float32)
         dx, dy, a11, a12, a21, a22 = zero, zero, one, zero, zero, one
         for k in range(planes):
-            parts = []
-            for side in range(2):
-                v = [view[k, j + side, pl.ds(TILE_R + i * TILE_R + n, TILE_R), :] for n in range(-3, 5)]
-                parts.append((
-                    sum(y0[b] * v[b + 2] for b in range(4)),
-                    sum(y1[b] * v[b] for b in range(8)),
-                    sum(y2[b] * v[b] for b in range(8)),
-                ))
-            f0, f1, f2 = [jnp.concatenate([parts[0][q], parts[1][q]], axis=1) for q in range(3)]
-            s0 = [f0[:, m + 1:m + 1 + TILE_C] for m in range(8)]
-            s1 = [f1[:, m + 1:m + 1 + TILE_C] for m in range(8)]
-            s2 = [f2[:, m + 3:m + 3 + TILE_C] for m in range(4)]
-            gx = sum(x1[m] * s0[m] for m in range(8))
-            xx = sum(x2[m] * s0[m] for m in range(8))
-            xy = sum(x1[m] * s1[m] for m in range(8))
-            gy = sum(x0[m] * s1[m + 2] for m in range(4))
-            yy = sum(x0[m] * s2[m] for m in range(4))
+            def row(q, n):
+                return field[fx + q, k, j, pl.ds(TILE_R + i * TILE_R + n, TILE_R), :]
+            plain = [row(0, n) for n in range(-3, 5)]
+            slope = [row(1, n) for n in range(-3, 5)]
+            curve = [row(2, n) for n in range(-1, 3)]
+            gx = sum(y0[b] * slope[b + 2] for b in range(4))
+            xx = sum(y0[b] * curve[b] for b in range(4))
+            xy = sum(y1[b] * slope[b] for b in range(8))
+            gy = sum(y1[b] * plain[b] for b in range(8))
+            yy = sum(y2[b] * plain[b] for b in range(8))
             lens = lens_ref[k]
             dx = dx + lens * gx
             dy = dy + lens * gy
@@ -261,7 +290,7 @@
         for n, a in enumerate((a11, a12, a21, a22)):
             distort_ref[n, 0, rs, at] = a
 
-    @pl.loop(0, ncols // TILE_C)
+    @pl.loop(0, tiles)
     def _(j):
         for i in range(nrows // TILE_R):
             tile(i, j)
@@ -307,24 +336,27 @@
     )(potential_stock, plane_pick, col_shift, mirror)
     f32 = jnp.float32
     nrows = subcell.shape[0] * TILE_R
+    filt = jnp.asarray(column_filters())
     return pl.pallas_call(
         trace_kernel,
         out_shape=(
             jax.ShapeDtypeStruct((2, 1, nrows, ncols), f32),
             jax.ShapeDtypeStruct((4, 1, nrows, ncols), f32),
         ),
-        in_specs=[sm, sm, sm, anyw, anyw, anyw],
+        in_specs=[sm, sm, sm, anyw, anyw, anyw, anyw],
         out_specs=(vm, vm),
         scratch_shapes=[
             pltpu.VMEM((planes, n, TILE_C), bf),
             pltpu.VMEM((planes, erows, TILE_C), bf),
             pltpu.VMEM((planes, erows, TILE_C), bf),
-            pltpu.VMEM((planes, out_tiles, nrows + 2 * TILE_R, TILE_C), f32),
+            pltpu.VMEM(filt.shape, bf),
+            pltpu.VMEM((planes, ncols // TILE_C + 1, TILE_R, TILE_C), f32),
+            pltpu.VMEM((SUB * 3, planes, ncols // TILE_C, nrows + 2 * TILE_R, TILE_C), f32),
             pltpu.SMEM((SUB, NTAB), f32),
-            dma((planes, 3)),
+            dma((planes, 3)), dma,
         ],
         name="trace",
-    )(plane_pick, subcell, lens_weight, main, before, after)
+    )(plane_pick, subcell, lens_weight, filt, main, before, after)
 
 
 def solution(mesh):

time: 73 us -> 42.6 us (0.58)
  Pallas kernels: 72.2 us -> 41.7 us
    pallas_call x1, Pallas kernels: 42.3 us -> 11.9 us  [body(): pl.pallas_call(trace_kernel, out_shape=(jax.ShapeDtypeStruct((2, 1, nrows...]
where the time goes in v2:
time: 42.6 us; the launch traced here: 42.4 us
  Pallas kernels  41.7 us (98%)
  between operations  0.64 us (2%)
    pallas_call x1, Pallas kernels, body(): pl.pallas_call(exchange_kernel, out_shape=(jax.ShapeDtypeStruct((peers, h...  29.9 us
    pallas_call x1, Pallas kernels, body(): pl.pallas_call(trace_kernel, out_shape=(jax.ShapeDtypeStruct((2, 1, nrows...  11.9 us

profile of v2, /device:TPU:0, one launch (start us, length us, event | category | flops | bytes accessed | tf_op | source)
XLA Modules:
  0.0 42.4 jit_solution(3646925120271881101)
XLA Ops:
  0.6 29.9 %exchange.1 = (bf16[4,2,544,128]{3,2,1,0:T(8,128)(2,1)}, bf16[4,2,80,128]{3,2,1,0:T(8,128)(2,1)}, bf16[4,2,80,128]{3,2,1,0:T(8,128)(2,1)}) custom-call(bf16[2,32,16384]{2,1,0:T(8,128)(2,1)} %stock_ref.1, s32[4]{0:T(128)} %pick_ref.3, s32[1,4]{1,0:T(1,128)} %shift_ref.1, s32[1,4]{1,0:T(1,128)} %mirror_ref.1), custom_call_target="tpu_custom_call" | custom-call | tf_op jit(solution)/shard_map/exchange/pallas_call | solution.py:312
  30.5 11.9 %trace.1 = (f32[2,1,32,2048]{3,2,1,0:T(8,128)}, f32[4,1,32,2048]{3,2,1,0:T(8,128)}) custom-call(s32[4]{0:T(128)} %pick_ref.3, s32[4,16]{1,0:T(4,128)} %subcell_ref.1, f32[4]{0:T(128)} %lens_ref.1, bf16[512,1536]{1,0:T(8,128)(2,1)} %constant.2.clone.filt_ref, bf16[4,2,544,128]{3,2,1,0:T(8,128)(2,1)} %get-tuple-element.5.main_ref, ...), custom_call_target="tpu_custom_call" | custom-call | tf_op jit(solution)/shard_map/trace/pallas_call | solution.py:340

commit v3 on v2

--- a/solution.py
+++ b/solution.py
@@ -67,8 +67,8 @@
     stock_t, tiles, send, edge32, esend, shifts_v, mirrors_v, shifts, mirrors,
     meta_send, meta_recv, local_sem, stock_sem, main_send, main_recv, edge_send, edge_recv,
 ):
-    held, rows, cols = stock_ref.shape
-    ntiles = cols // TILE_C
+    held, blocks, ntiles = stock_ref.shape[:3]
+    rows, cols = blocks * TILE_R, ntiles * TILE_C
     out_tiles = main_ref.shape[2] // rows
     planes = pick_ref.shape[0]
     peers = lax.axis_size("real")
@@ -78,13 +78,8 @@
     above = lax.rem(strip + strips - 1, strips)
     below = lax.rem(strip + 1, strips)
 
-    for e in range(held):
-        @pl.loop(0, ntiles)
-        def _(t):
-            at = pl.ds(pl.multiple_of(t * TILE_C, TILE_C), TILE_C)
-            pltpu.make_async_copy(
-                stock_ref.at[e, :, at], stock_t.at[e * ntiles + t], stock_sem).start()
-
+    stock_copy = pltpu.make_async_copy(stock_ref, stock_t, stock_sem)
+    stock_copy.start()
     barrier = pltpu.get_barrier_semaphore()
     for off in range(peers):
         r = lax.rem(me + off, peers)
@@ -158,8 +153,9 @@
             base = lax.div(start, TILE_C)
             inner = start - base * TILE_C
             for u in range(out_tiles + 1):
-                at = e * ntiles + lax.rem(base + step * u + ntiles, ntiles)
-                tiles[u * rows:(u + 1) * rows, :] = stock_t[at]
+                at = lax.rem(base + step * u + ntiles, ntiles)
+                for b in range(blocks):
+                    tiles[u * rows + b * TILE_R:u * rows + (b + 1) * TILE_R, :] = stock_t[e, b, at]
             near = lane_in == inner + step * lane_out
             far = lane_in - TILE_C == inner + step * (lane_out - TILE_C)
             choose = ((near & (lane_in < TILE_C)) | (far & (lane_in >= TILE_C)))
@@ -174,7 +170,7 @@
             esend[off, 0, e] = edge32[0].astype(jnp.bfloat16)
             esend[off, 1, e] = edge32[1].astype(jnp.bfloat16)
 
-    pltpu.make_async_copy(stock_t, stock_t, stock_sem).wait()
+    stock_copy.wait()
     edge32[...] = jnp.zeros_like(edge32)
     order = sorted(range(1, peers), key=lambda off: abs(2 * off - peers)) + [0]
     for off in order:
@@ -197,7 +193,7 @@
 def trace_kernel(
     pick_ref, subcell_ref, lens_ref, filt_ref, main_ref, before_ref, after_ref,
     deflect_ref, distort_ref,
-    main_v, before_v, after_v, filt_v, edges, field, table, sems, filt_sem,
+    main_v, before_v, after_v, filt_v, edges, pairs, field, table, sems, filt_sem,
 ):
     planes = pick_ref.shape[0]
     held = main_ref.shape[1]
@@ -231,26 +227,30 @@
         for t in range(tiles + 1):
             edges[k, t, EDGE:2 * EDGE, :] = up[t * EDGE:(t + 1) * EDGE]
             edges[k, t, 0:EDGE, :] = down[t * EDGE:(t + 1) * EDGE]
+
+    m = tiles * nrows
+    for k in range(planes):
+        flank = edges[k]
+        for side in range(2):
+            lanes = slice(side * TILE_C, (side + 1) * TILE_C)
+            pairs[k, 0:m, lanes] = main_v[k, side * nrows:m + side * nrows, :]
+            pairs[k, m:m + tiles * TILE_R, lanes] = flank[side:tiles + side].reshape(
+                tiles * TILE_R, TILE_C).astype(jnp.bfloat16)
     filt_copy.wait()
 
-    @pl.loop(0, planes)
-    def _(k):
-        m = tiles * nrows
-        flank = edges[k]
-        near = jnp.concatenate(
-            [main_v[k, 0:m, :], flank[0:tiles].reshape(tiles * TILE_R, TILE_C).astype(jnp.bfloat16)], axis=0)
-        far = jnp.concatenate(
-            [main_v[k, nrows:m + nrows, :], flank[1:tiles + 1].reshape(tiles * TILE_R, TILE_C).astype(jnp.bfloat16)],
-            axis=0)
-        lhs = jnp.concatenate([near, far, near, far], axis=1)
-        for c in range(0, nfilt, 2):
-            got = jnp.dot(lhs, filt_v[:, c * TILE_C:(c + 2) * TILE_C], preferred_element_type=jnp.float32)
+    @pl.loop(0, nfilt // 2)
+    def _(c):
+        cols = pl.ds(pl.multiple_of(c * 2 * TILE_C, 2 * TILE_C), 2 * TILE_C)
+        filt = filt_v[:, cols]
+        for k in range(planes):
+            lhs = pairs[k]
+            got = jnp.dot(jnp.concatenate([lhs, lhs], axis=1), filt, preferred_element_type=jnp.float32)
             for h in range(2):
                 part = got[:, h * TILE_C:(h + 1) * TILE_C]
                 ends = part[m:].reshape(tiles, TILE_R, TILE_C)
-                field[c + h, k, :, TILE_R:TILE_R + nrows, :] = part[:m].reshape(tiles, nrows, TILE_C)
-                field[c + h, k, :, 0:TILE_R, :] = ends
-                field[c + h, k, :, TILE_R + nrows:2 * TILE_R + nrows, :] = ends
+                field[2 * c + h, k, :, TILE_R:TILE_R + nrows, :] = part[:m].reshape(tiles, nrows, TILE_C)
+                field[2 * c + h, k, :, 0:TILE_R, :] = ends
+                field[2 * c + h, k, :, TILE_R + nrows:2 * TILE_R + nrows, :] = ends
 
     def tile(i, j):
         o = subcell_ref[i, j]
@@ -304,6 +304,8 @@
     out_tiles = -(-(ncols + 2 * EDGE) // TILE_C)
     erows = -(-(out_tiles * EDGE) // 16) * 16
     n = out_tiles * rows
+    stock = potential_stock.reshape(held, rows // TILE_R, TILE_R, cols // TILE_C, TILE_C)
+    stock = stock.transpose(0, 1, 3, 2, 4)
     vm = pl.BlockSpec(memory_space=pltpu.VMEM)
     sm = pl.BlockSpec(memory_space=pltpu.SMEM)
     anyw = pl.BlockSpec(memory_space=pl.ANY)
@@ -319,7 +321,7 @@
         in_specs=[anyw, sm, vm, vm],
         out_specs=(anyw, anyw, anyw),
         scratch_shapes=[
-            pltpu.VMEM((held * (cols // TILE_C), rows, TILE_C), bf),
+            pltpu.VMEM(stock.shape, bf),
             pltpu.VMEM((n + rows, TILE_C), bf),
             pltpu.VMEM((peers, held, n, TILE_C), bf),
             pltpu.VMEM((2, erows, TILE_C), jnp.float32),
@@ -333,7 +335,7 @@
         ],
         compiler_params=pltpu.CompilerParams(collective_id=0, has_side_effects=True),
         name="exchange",
-    )(potential_stock, plane_pick, col_shift, mirror)
+    )(stock, plane_pick, col_shift, mirror)
     f32 = jnp.float32
     nrows = subcell.shape[0] * TILE_R
     filt = jnp.asarray(column_filters())
@@ -351,6 +353,7 @@
             pltpu.VMEM((planes, erows, TILE_C), bf),
             pltpu.VMEM(filt.shape, bf),
             pltpu.VMEM((planes, ncols // TILE_C + 1, TILE_R, TILE_C), f32),
+            pltpu.VMEM((planes, (ncols // TILE_C) * (nrows + TILE_R), 2 * TILE_C), bf),
             pltpu.VMEM((SUB * 3, planes, ncols // TILE_C, nrows + 2 * TILE_R, TILE_C), f32),
             pltpu.SMEM((SUB, NTAB), f32),
             dma((planes, 3)), dma,

time: 42.6 us -> 40.6 us (0.953)
  Pallas kernels: 41.7 us -> 39.7 us
    pallas_call x1, Pallas kernels: 29.9 us -> 27.5 us  [body(): pl.pallas_call(exchange_kernel, out_shape=(jax.ShapeDtypeStruct((peers, h...]
where the time goes in v3:
time: 40.6 us; the launch traced here: 40.4 us
  Pallas kernels  39.7 us (98%)
  between operations  0.64 us (2%)
    pallas_call x1, Pallas kernels, body(): pl.pallas_call(exchange_kernel, out_shape=(jax.ShapeDtypeStruct((peers, h...  27.5 us
    pallas_call x1, Pallas kernels, body(): pl.pallas_call(trace_kernel, out_shape=(jax.ShapeDtypeStruct((2, 1, nrows...  12.2 us

profile of v3, /device:TPU:0, one launch (start us, length us, event | category | flops | bytes accessed | tf_op | source)
XLA Modules:
  0.0 40.4 jit_solution(2039658655014973091)
XLA Ops:
  0.6 27.5 %exchange.1 = (bf16[4,2,544,128]{3,2,1,0:T(8,128)(2,1)}, bf16[4,2,80,128]{3,2,1,0:T(8,128)(2,1)}, bf16[4,2,80,128]{3,2,1,0:T(8,128)(2,1)}) custom-call(bf16[2,4,128,8,128]{4,3,2,1,0:T(8,128)(2,1)} %bitcast.3, s32[4]{0:T(128)} %pick_ref.3, s32[1,4]{1,0:T(1,128)} %shift_ref.1, s32[1,4]{1,0:T(1,128)} %mirror_ref.1), custom_call_target="tpu_custom_call" | custom-call | tf_op jit(solution)/shard_map/exchange/pallas_call | solution.py:314
  28.1 12.2 %trace.1 = (f32[2,1,32,2048]{3,2,1,0:T(8,128)}, f32[4,1,32,2048]{3,2,1,0:T(8,128)}) custom-call(s32[4]{0:T(128)} %pick_ref.3, s32[4,16]{1,0:T(4,128)} %subcell_ref.1, f32[4]{0:T(128)} %lens_ref.1, bf16[512,1536]{1,0:T(8,128)(2,1)} %constant.2.clone.filt_ref, bf16[4,2,544,128]{3,2,1,0:T(8,128)(2,1)} %get-tuple-element.5.main_ref, ...), custom_call_target="tpu_custom_call" | custom-call | tf_op jit(solution)/shard_map/trace/pallas_call | solution.py:342

commit v4 on v3

--- a/solution.py
+++ b/solution.py
@@ -193,7 +193,7 @@
 def trace_kernel(
     pick_ref, subcell_ref, lens_ref, filt_ref, main_ref, before_ref, after_ref,
     deflect_ref, distort_ref,
-    main_v, before_v, after_v, filt_v, edges, pairs, field, table, sems, filt_sem,
+    main_v, before_v, after_v, filt_v, edges, pairs, field_a, field_b, table, sems, filt_sem,
 ):
     planes = pick_ref.shape[0]
     held = main_ref.shape[1]
@@ -238,21 +238,28 @@
                 tiles * TILE_R, TILE_C).astype(jnp.bfloat16)
     filt_copy.wait()
 
-    @pl.loop(0, nfilt // 2)
-    def _(c):
-        cols = pl.ds(pl.multiple_of(c * 2 * TILE_C, 2 * TILE_C), 2 * TILE_C)
-        filt = filt_v[:, cols]
-        for k in range(planes):
-            lhs = pairs[k]
-            got = jnp.dot(jnp.concatenate([lhs, lhs], axis=1), filt, preferred_element_type=jnp.float32)
-            for h in range(2):
-                part = got[:, h * TILE_C:(h + 1) * TILE_C]
-                ends = part[m:].reshape(tiles, TILE_R, TILE_C)
-                field[2 * c + h, k, :, TILE_R:TILE_R + nrows, :] = part[:m].reshape(tiles, nrows, TILE_C)
-                field[2 * c + h, k, :, 0:TILE_R, :] = ends
-                field[2 * c + h, k, :, TILE_R + nrows:2 * TILE_R + nrows, :] = ends
+    span = field_a.shape[2]
+    fields = (field_a, field_b)
+
+    def filter_pair(g, c):
+        field = fields[g % 2]
+        mains = slice(g * span * nrows, (g + 1) * span * nrows)
+        flanks = slice(m + g * span * TILE_R, m + (g + 1) * span * TILE_R)
+        lhs = jnp.concatenate(
+            [pairs[k, mains, :] for k in range(planes)] + [pairs[k, flanks, :] for k in range(planes)], axis=0)
+        got = jnp.dot(
+            jnp.concatenate([lhs, lhs], axis=1), filt_v[:, 2 * c * TILE_C:2 * (c + 1) * TILE_C],
+            preferred_element_type=jnp.float32)
+        for h in range(2):
+            part = got[:, h * TILE_C:(h + 1) * TILE_C]
+            body_rows = part[:planes * span * nrows].reshape(planes, span, nrows, TILE_C)
+            ends = part[planes * span * nrows:].reshape(planes, span, TILE_R, TILE_C)
+            field[2 * c + h, :, :, TILE_R:TILE_R + nrows, :] = body_rows
+            field[2 * c + h, :, :, 0:TILE_R, :] = ends
+            field[2 * c + h, :, :, TILE_R + nrows:2 * TILE_R + nrows, :] = ends
 
     def tile(i, j):
+        field, jj = fields[(j // span) % 2], j % span
         o = subcell_ref[i, j]
         oy = o // SUB
         fx = (o - oy * SUB) * 3
@@ -264,7 +271,7 @@
         dx, dy, a11, a12, a21, a22 = zero, zero, one, zero, zero, one
         for k in range(planes):
             def row(q, n):
-                return field[fx + q, k, j, pl.ds(TILE_R + i * TILE_R + n, TILE_R), :]
+                return field[fx + q, k, jj, pl.ds(TILE_R + i * TILE_R + n, TILE_R), :]
             plain = [row(0, n) for n in range(-3, 5)]
             slope = [row(1, n) for n in range(-3, 5)]
             curve = [row(2, n) for n in range(-1, 3)]
@@ -283,17 +290,25 @@
                 a21 - (xy * a11 + yy * a21),
                 a22 - (xy * a12 + yy * a22),
             )
-        at = pl.ds(pl.multiple_of(j * TILE_C, TILE_C), TILE_C)
+        at = slice(j * TILE_C, (j + 1) * TILE_C)
         rs = slice(i * TILE_R, (i + 1) * TILE_R)
         deflect_ref[0, 0, rs, at] = dx
         deflect_ref[1, 0, rs, at] = dy
         for n, a in enumerate((a11, a12, a21, a22)):
             distort_ref[n, 0, rs, at] = a
 
-    @pl.loop(0, tiles)
-    def _(j):
-        for i in range(nrows // TILE_R):
-            tile(i, j)
+    groups = tiles // span
+    npairs = nfilt // 2
+    for c in range(npairs):
+        filter_pair(0, c)
+    for g in range(groups):
+        todo = [(i, g * span + jj) for jj in range(span) for i in range(nrows // TILE_R)]
+        each = -(-len(todo) // npairs)
+        for c in range(npairs):
+            if g + 1 < groups:
+                filter_pair(g + 1, c)
+            for i, j in todo[c * each:(c + 1) * each]:
+                tile(i, j)
 
 
 def body(potential_stock, plane_pick, col_shift, mirror, subcell, lens_weight):
@@ -338,6 +353,8 @@
     )(stock, plane_pick, col_shift, mirror)
     f32 = jnp.float32
     nrows = subcell.shape[0] * TILE_R
+    tiles = ncols // TILE_C
+    span = next(d for d in (4, 3, 2, 1) if tiles % d == 0)
     filt = jnp.asarray(column_filters())
     return pl.pallas_call(
         trace_kernel,
@@ -354,7 +371,8 @@
             pltpu.VMEM(filt.shape, bf),
             pltpu.VMEM((planes, ncols // TILE_C + 1, TILE_R, TILE_C), f32),
             pltpu.VMEM((planes, (ncols // TILE_C) * (nrows + TILE_R), 2 * TILE_C), bf),
-            pltpu.VMEM((SUB * 3, planes, ncols // TILE_C, nrows + 2 * TILE_R, TILE_C), f32),
+            pltpu.VMEM((SUB * 3, planes, span, nrows + 2 * TILE_R, TILE_C), f32),
+            pltpu.VMEM((SUB * 3, planes, span, nrows + 2 * TILE_R, TILE_C), f32),
             pltpu.SMEM((SUB, NTAB), f32),
             dma((planes, 3)), dma,
         ],

time: 40.6 us -> 38.1 us (0.938)
  Pallas kernels: 39.7 us -> 37.3 us
    pallas_call x1, Pallas kernels: 12.2 us -> 9.74 us  [body(): pl.pallas_call(trace_kernel, out_shape=(jax.ShapeDtypeStruct((2, 1, nrows...]
where the time goes in v4:
time: 38.1 us; the launch traced here: 37.9 us
  Pallas kernels  37.3 us (98%)
  between operations  0.64 us (2%)
    pallas_call x1, Pallas kernels, body(): pl.pallas_call(exchange_kernel, out_shape=(jax.ShapeDtypeStruct((peers, h...  27.5 us
    pallas_call x1, Pallas kernels, body(): pl.pallas_call(trace_kernel, out_shape=(jax.ShapeDtypeStruct((2, 1, nrows...  9.74 us

profile of v4, /device:TPU:0, one launch (start us, length us, event | category | flops | bytes accessed | tf_op | source)
XLA Modules:
  0.0 37.9 jit_solution(9076587728229986043)
XLA Ops:
  0.6 27.5 %exchange.1 = (bf16[4,2,544,128]{3,2,1,0:T(8,128)(2,1)}, bf16[4,2,80,128]{3,2,1,0:T(8,128)(2,1)}, bf16[4,2,80,128]{3,2,1,0:T(8,128)(2,1)}) custom-call(bf16[2,4,128,8,128]{4,3,2,1,0:T(8,128)(2,1)} %bitcast.3, s32[4]{0:T(128)} %pick_ref.3, s32[1,4]{1,0:T(1,128)} %shift_ref.1, s32[1,4]{1,0:T(1,128)} %mirror_ref.1), custom_call_target="tpu_custom_call" | custom-call | tf_op jit(solution)/shard_map/exchange/pallas_call | solution.py:329
  28.1 9.7 %trace.1 = (f32[2,1,32,2048]{3,2,1,0:T(8,128)}, f32[4,1,32,2048]{3,2,1,0:T(8,128)}) custom-call(s32[4]{0:T(128)} %pick_ref.3, s32[4,16]{1,0:T(4,128)} %subcell_ref.1, f32[4]{0:T(128)} %lens_ref.1, bf16[512,1536]{1,0:T(8,128)(2,1)} %constant.2.clone.filt_ref, bf16[4,2,544,128]{3,2,1,0:T(8,128)(2,1)} %get-tuple-element.5.main_ref, ...), custom_call_target="tpu_custom_call" | custom-call | tf_op jit(solution)/shard_map/trace/pallas_call | solution.py:359
